TPU v7x, 32 devices: a whole 2x2x4 slice. The times are simulated.
32 devices in a mesh: shard: 2 (over y), blk: 4 (over z), ckpt: 2 (over x), qry: 2 (over core).
Axes of the slice: x: 2, y: 2, z: 4, core: 2. Of those that a mesh axis runs over, the one named last changes fastest.
Arguments:
- query_feats: bfloat16 [2, 8192, 2048], P('ckpt', ('shard', 'blk', 'qry')), parts along dimension 1, may hold values from -6 to 6
- train_feats: bfloat16 [2, 1024, 2048], P('ckpt', ('shard', 'blk')), parts along dimension 1, may hold values from -0.125 to 0.125
- loss_weights: bfloat16 [2, 1024], P('ckpt', ('shard', 'blk')), parts along dimension 1, may hold values from 0.099609375 to 1
- pair_list: int32 [32, 2], P(('shard', 'blk', 'qry')), parts along dimension 0, may hold values from 0 to 3, all different within a row
- tile_owner: int32 [8], P('shard'), parts along dimension 0, may hold values from 0 to 3, each once
Outputs:
- scores: float32 [8192, 512], P(('shard', 'blk', 'qry'), 'ckpt'), parts along dimension 0
There are 2 independent parts, one for each index of `shard`. A program takes and returns all parts, laid end to end along the dimension named above; each array names one. Nothing has to cross between parts.
Inputs may be any that keep to these rules, and one draw needn't show every extreme that they name: `pair_list`: each row names 2 different training blocks; every training block is named by some row. `tile_owner`: a permutation of the training blocks.
All inputs are finite; a program needn't handle non-finite values.
Results may differ from a plain program's by a relative error of at most 0.0003.
Values may be sent and summed in bfloat16 or wider, within the bound.
No kernel may reach another device: no remote copies, remote signals or barrier semaphores. Data moves between devices by JAX's collectives and lax.ppermute only.
A program may use at most 128 MiB of HBM per device.

v0:
```python
import jax
import jax.numpy as jnp
from jax import lax
from jax.sharding import PartitionSpec as P

QBLK = 256
TBLK = 128


def per_device(query_feats, train_feats, loss_weights, pair_list, tile_owner):
    queries = query_feats[0]
    block_count = lax.axis_size("blk")
    total_rows = TBLK * block_count
    block_ids = jnp.arange(block_count, dtype=jnp.int32)
    wanted = jnp.any(pair_list[:, :, None] == block_ids[None, None, :], axis=1).astype(jnp.float32)
    own_rows = train_feats[0]
    own_weights = loss_weights[0]
    gathered_rows, gathered_weights = (
        lax.all_gather(own_rows, "blk", axis=0, tiled=True),
        lax.all_gather(own_weights, "blk", axis=0, tiled=True),
    )
    row_blocks = gathered_rows.reshape(block_count, TBLK, gathered_rows.shape[1])
    weight_blocks = gathered_weights.reshape(block_count, TBLK)
    query_mask = jnp.transpose(jnp.repeat(wanted, QBLK, axis=0))
    owner_rows = total_rows // lax.axis_size("ckpt")
    picked = row_blocks[tile_owner].reshape(lax.axis_size("ckpt") * owner_rows, row_blocks.shape[2])
    picked_weights = (
        weight_blocks[tile_owner].reshape(lax.axis_size("ckpt") * owner_rows).astype(jnp.float32)
    )
    products = lax.dot_general(
        picked, queries, (((1,), (1,)), ((), ())), preferred_element_type=jnp.float32
    )
    mask_rows = jnp.repeat(query_mask[tile_owner], TBLK, axis=0)
    summed_rows = lax.psum_scatter(
        products * picked_weights[:, None] * mask_rows, "ckpt", scatter_dimension=0, tiled=True
    )
    return jnp.transpose(summed_rows)


def solution(mesh):
    return jax.shard_map(
        per_device,
        mesh=mesh,
        in_specs=(
            P("ckpt", ("shard", "blk", "qry"), None),
            P("ckpt", ("shard", "blk"), None),
            P("ckpt", ("shard", "blk")),
            P(("shard", "blk", "qry"), None),
            P("shard"),
        ),
        out_specs=P(("shard", "blk", "qry"), "ckpt"),
        check_vma=False,
    )
```

profile of v0, /device:TPU:0, one launch (start us, length us, event | category | flops | bytes accessed | tf_op | source)
XLA Modules:
  0.0 93.2 jit_solution(14550216381288683997)
XLA Ops:
  6.5 0.0 copy-start
  6.5 0.0 all-gather.4.cloned.1.call-start
  6.5 0.7 all-gather.4.cloned.1.call-update
  7.3 0.0 reduce-scatter.2.cloned.1.call-start
  7.3 0.8 compare_reduce_fusion
  8.1 0.1 copy.7
  8.2 0.1 broadcast_bitcast_fusion
  8.3 0.7 compare_select_fusion
  8.9 0.6 gather_fusion.2
  9.5 12.8 %all-gather.1 = bf16[1,512]{1,0:T(2,128)(2,1)S(1)} all-gather(bf16[1,128]{1,0:T(2,128)(2,1)} %param.7), channel_id=3, replica_groups=mesh['shard'=2,'blk'=4,'ckpt'=2,'qry'=2] {'blk'}, dimensions={1}, use_global_device_ids=true | all-gather | bytes 1280 | tf_op jit(solution)/shard_map/all_gather | solution.py:20
  22.3 0.6 gather_fusion.1
  22.9 34.4 %all-gather.4.cloned.1.call-done = bf16[1,512,2048]{2,1,0:T(8,128)(2,1)} async-done(((bf16[1,128,2048]{2,1,0:T(8,128)(2,1)}), bf16[1,512,2048]{2,1,0:T(8,128)(2,1)}) %all-gather.4.cloned.1.call-update) | async-done | bytes 2097168 | tf_op jit(solution)/shard_map/all_gather | solution.py:19
  57.3 3.6 %gather_fusion = bf16[4,128,2048]{2,1,0:T(8,128)(2,1)} fusion(bf16[4,128,2048]{2,1,0:T(8,128)(2,1)} %bitcast.23, s32[1024]{0:T(1024)S(1)} %pad_clamp_fusion), kind=kCustom, calls=%fused_computation | custom fusion | bytes 4194320 | tf_op jit(solution)/shard_map/gather | solution.py:26
  60.9 0.1 broadcast_in_dim.16
  61.1 0.0 copy-done
  61.1 3.9 %fusion.5 = f32[512,512]{1,0:T(8,128)} fusion(f32[512,512]{1,0:T(8,128)S(1)} %bitcast.25, bf16[512,2048]{1,0:T(8,128)(2,1)} %bitcast.24, bf16[1,512,2048]{2,1,0:T(8,128)(2,1)S(1)} %copy-done, f32[512]{0:T(512)S(1)} %bitcast_convert_fusion), kind=kOutput, calls=%fused_computation.6 | convolution fusion | flops 1074266112 | bytes 6293504 | tf_op jit(solution)/shard_map/dot_general | solution.py:30
  64.9 0.0 reduce-scatter.2.cloned.1.call-update
  65.0 19.3 %reduce-scatter.2.cloned.1.call-done = f32[256,512]{1,0:T(8,128)} async-done(((f32[512,512]{1,0:T(8,128)}), f32[256,512]{1,0:T(8,128)}) %reduce-scatter.2.cloned.1.call-update) | async-done | bytes 524304 | tf_op jit(solution)/shard_map/reduce_scatter | solution.py:34
  84.3 2.0 %copy.8 = f32[512,256]{1,0:T(8,128)} copy(f32[512,256]{0,1:T(8,128)} %bitcast.27) | data formatting | bytes 1048576 | tf_op jit(solution)/shard_map/transpose | solution.py:37
  (5 shorter events, 0.0 us)
Async XLA Ops:
  6.5 54.5 %copy-start = (bf16[1,512,2048]{2,1,0:T(8,128)(2,1)S(1)}, bf16[1,512,2048]{2,1,0:T(8,128)(2,1)}, u32[]{:S(2)}) copy-start(bf16[1,512,2048]{2,1,0:T(8,128)(2,1)} %param.5) | copy-start | bytes 6291460
  6.5 50.8 %all-gather.4.cloned.1.call-start = ((), (), s32[]{:S(2)}) async-start(), calls=%async_computation.2 | async-start | bytes 2621440 | tf_op jit(solution)/shard_map/all_gather | solution.py:19
  7.3 77.0 %reduce-scatter.2.cloned.1.call-start = ((), (), s32[]{:S(2)}) async-start(), calls=%async_computation.1 | async-start | bytes 1572864 | tf_op jit(solution)/shard_map/reduce_scatter | solution.py:34
Sparse Core Ops, SparseCore 0:
  8.9 48.3 all-gather.3
  65.1 19.1 reduce-scatter.1
where the time goes:
time: 93.4 us; the launch traced here: 93.2 us
  waiting for transfers between devices  54.5 us (58%)
  between operations  13.4 us (14%)
  blocking collectives  12.8 us (14%)
  local copies, waits for them, and re-layouts  7.07 us (8%)
  matrix products  3.86 us (4%)
  other arithmetic  1.47 us (2%)
    all_gather x1, waiting for transfers between devices, per_device(): lax.all_gather(own_rows, 'blk', axis=0, tiled=True)  34.4 us
    reduce_scatter x1, waiting for transfers between devices, per_device(): lax.psum_scatter(products * picked_weights[:, None] * mask_rows, 'ckpt',...  19.3 us
    all_gather x1, blocking collectives, per_device(): lax.all_gather(own_weights, 'blk', axis=0, tiled=True)  12.8 us
    dot_general x1, matrix products, per_device(): lax.dot_general(picked, queries, (((1,), (1,)), ((), ())), preferred_elem...  3.86 us
    gather x1, local copies, waits for them, and re-layouts, per_device(): row_blocks[tile_owner]  3.62 us
    transpose x1, local copies, waits for them, and re-layouts, per_device(): return jnp.transpose(summed_rows)  2.04 us
  transfers between devices with their start and end apart: 2, of which 2 were waited for; matrix products, arithmetic and copies ran while one was open for 3% of the time, Pallas kernels for 0%

commit v1 on v0

--- a/solution.py
+++ b/solution.py
@@ -5,6 +5,17 @@
 
 QBLK = 256
 TBLK = 128
+
+
+def gather_around(value, axis, dim):
+    ways = lax.axis_size(axis)
+    pieces = [value]
+    for far in range(1, ways):
+        pieces.append(
+            lax.ppermute(pieces[far - 1], axis, [(d, (d - 1) % ways) for d in range(ways)])
+        )
+    line = jnp.concatenate(pieces, axis=dim)
+    return jnp.roll(line, lax.axis_index(axis) * value.shape[dim], axis=dim)
 
 
 def per_device(query_feats, train_feats, loss_weights, pair_list, tile_owner):
@@ -16,7 +27,7 @@
     own_rows = train_feats[0]
     own_weights = loss_weights[0]
     gathered_rows, gathered_weights = (
-        lax.all_gather(own_rows, "blk", axis=0, tiled=True),
+        gather_around(own_rows, "blk", 0),
         lax.all_gather(own_weights, "blk", axis=0, tiled=True),
     )
     row_blocks = gathered_rows.reshape(block_count, TBLK, gathered_rows.shape[1])

time: 93.4 us -> 105 us (1.12)
  waiting for transfers between devices: 54.5 us -> 38.2 us
  local copies, waits for them, and re-layouts: 7.07 us -> 22.3 us
  starting transfers between devices: 0.04 us -> 9.26 us
  blocking collectives: 12.8 us -> 16.3 us
    all_gather x1 -> x0, waiting for transfers between devices: 34.4 us -> none  [per_device(): lax.all_gather(own_rows, 'blk', axis=0, tiled=True)]
    ppermute x0 -> x3, waiting for transfers between devices: none -> 17.9 us  [gather_around(): lax.ppermute(pieces[far - 1], axis, [(d, (d - 1) % ways) for d in range(w...]
    unnamed x4 -> x13, local copies, waits for them, and re-layouts: 0.08 us -> 10.2 us
    ppermute x0 -> x3, starting transfers between devices: none -> 9.25 us  [gather_around(): lax.ppermute(pieces[far - 1], axis, [(d, (d - 1) % ways) for d in range(w...]
    all_gather x1, blocking collectives: 12.8 us -> 16.3 us  [per_device(): lax.all_gather(own_weights, 'blk', axis=0, tiled=True)]
    dynamic_slice x0 -> x1, local copies, waits for them, and re-layouts: none -> 3.17 us  [gather_around(): return jnp.roll(line, lax.axis_index(axis) * value.shape[dim], axis=dim)]
    concatenate x0 -> x1, local copies, waits for them, and re-layouts: none -> 1.9 us  [gather_around(): return jnp.roll(line, lax.axis_index(axis) * value.shape[dim], axis=dim)]
  transfers between devices with their start and end apart: 2 -> 4, of which waited for: 2 -> 3; matrix products, arithmetic and copies ran while one was open for 3% -> 7% of each run, Pallas kernels for 0% -> 0%
where the time goes in v1:
time: 105 us
  waiting for transfers between devices  38.2 us (36%)
  local copies, waits for them, and re-layouts  22.3 us (21%)
  blocking collectives  16.3 us (16%)
  between operations  13.5 us (13%)
  starting transfers between devices  9.26 us (9%)
  matrix products  3.86 us (4%)
  other arithmetic  1.46 us (1%)
    reduce_scatter x1, waiting for transfers between devices, per_device(): lax.psum_scatter(products * picked_weights[:, None] * mask_rows, 'ckpt',...  20.3 us
    ppermute x3, waiting for transfers between devices, gather_around(): lax.ppermute(pieces[far - 1], axis, [(d, (d - 1) % ways) for d in range(w...  17.9 us
    all_gather x1, blocking collectives, per_device(): lax.all_gather(own_weights, 'blk', axis=0, tiled=True)  16.3 us
    unnamed x13, local copies, waits for them, and re-layouts  10.2 us
    ppermute x3, starting transfers between devices, gather_around(): lax.ppermute(pieces[far - 1], axis, [(d, (d - 1) % ways) for d in range(w...  9.25 us
    dot_general x1, matrix products, per_device(): lax.dot_general(picked, queries, (((1,), (1,)), ((), ())), preferred_elem...  3.86 us
    gather x1, local copies, waits for them, and re-layouts, per_device(): row_blocks[tile_owner]  3.62 us
    dynamic_slice x1, local copies, waits for them, and re-layouts, gather_around(): return jnp.roll(line, lax.axis_index(axis) * value.shape[dim], axis=dim)  3.17 us
  transfers between devices with their start and end apart: 4, of which 3 were waited for; matrix products, arithmetic and copies ran while one was open for 7% of the time, Pallas kernels for 0%

profile of v1, /device:TPU:0, one launch (start us, length us, event | category | flops | bytes accessed | tf_op | source)
XLA Modules:
  0.0 104.8 jit_solution(15724882012996473232)
XLA Ops:
  6.5 0.0 copy-start
  6.5 0.0 reduce-scatter.2.cloned.1.call-start
  6.5 5.1 %collective-permute-start = (bf16[128,2048]{1,0:T(8,128)(2,1)}, bf16[128,2048]{1,0:T(8,128)(2,1)S(1)}, u32[]{:S(2)}, u32[]{:S(2)}) collective-permute-start(bf16[128,2048]{1,0:T(8,128)(2,1)} %bitcast.28), channel_id=1, source_target_pairs={{0,12},{4,0},{8,4},{12,8},{1,13},{5,1},{9,5},{13,9},{2,14},{6,2},{... | collective-permute-start | bytes 1572872 | tf_op jit(solution)/shard_map/ppermute | solution.py:15
  11.6 0.8 compare_reduce_fusion
  12.4 0.1 copy.7
  12.5 0.7 compare_select_fusion
  13.1 0.1 broadcast_bitcast_fusion
  13.2 9.9 %collective-permute-done = bf16[128,2048]{1,0:T(8,128)(2,1)S(1)} collective-permute-done((bf16[128,2048]{1,0:T(8,128)(2,1)}, bf16[128,2048]{1,0:T(8,128)(2,1)S(1)}, u32[]{:S(2)}, u32[]{:S(2)}) %collective-permute-start) | collective-permute-done | bytes 524320 | tf_op jit(solution)/shard_map/ppermute | solution.py:15
  23.1 4.2 %collective-permute-start.1 = (bf16[128,2048]{1,0:T(8,128)(2,1)S(1)}, bf16[128,2048]{1,0:T(8,128)(2,1)}, u32[]{:S(2)}, u32[]{:S(2)}) collective-permute-start(bf16[128,2048]{1,0:T(8,128)(2,1)S(1)} %collective-permute-done), channel_id=1, source_target_pairs={{0,12},{4,0},{8,4},{12,8},{1,13},{5,1},{9,5},{13,9},{2,14},{6,2},{... | collective-permute-start | bytes 1572872 | tf_op jit(solution)/shard_map/ppermute | solution.py:15
  27.3 16.3 %all-gather = bf16[1,512]{1,0:T(2,128)(2,1)S(1)} all-gather(bf16[1,128]{1,0:T(2,128)(2,1)} %param.7), channel_id=2, replica_groups=mesh['shard'=2,'blk'=4,'ckpt'=2,'qry'=2] {'blk'}, dimensions={1}, use_global_device_ids=true | all-gather | bytes 1280 | tf_op jit(solution)/shard_map/all_gather | solution.py:31
  43.6 0.6 gather_fusion.1
  44.2 1.9 %constant_dynamic-update-slice_fusion.7 = bf16[1024,2048]{1,0:T(8,128)(2,1)} fusion(bf16[1,128,2048]{2,1,0:T(8,128)(2,1)} %param.6), kind=kLoop, calls=%fused_computation.14 | loop fusion | bytes 1048576
  46.0 0.0 collective-permute-done.1
  46.0 0.0 collective-permute-start.2
  46.1 0.6 gather_fusion.2
  46.6 0.9 constant_dynamic-update-slice_fusion.6
  47.5 1.9 %constant_dynamic-update-slice_fusion.5 = bf16[1024,2048]{1,0:T(8,128)(2,1)} fusion(bf16[1024,2048]{1,0:T(8,128)(2,1)} %constant_dynamic-update-slice_fusion.6, bf16[128,2048]{1,0:T(8,128)(2,1)} %collective-permute-done.1), kind=kLoop, calls=%fused_computation.12 | loop fusion | bytes 1048576
  49.4 8.0 %collective-permute-done.2 = bf16[128,2048]{1,0:T(8,128)(2,1)} collective-permute-done((bf16[128,2048]{1,0:T(8,128)(2,1)}, bf16[128,2048]{1,0:T(8,128)(2,1)}, u32[]{:S(2)}, u32[]{:S(2)}) %collective-permute-start.2) | collective-permute-done | bytes 524320 | tf_op jit(solution)/shard_map/ppermute | solution.py:15
  57.4 1.9 %constant_dynamic-update-slice_fusion.4 = bf16[1024,2048]{1,0:T(8,128)(2,1)} fusion(bf16[1024,2048]{1,0:T(8,128)(2,1)} %constant_dynamic-update-slice_fusion.5, bf16[128,2048]{1,0:T(8,128)(2,1)} %collective-permute-done.2), kind=kLoop, calls=%fused_computation.11 | loop fusion | bytes 1048576
  59.3 0.0 copy-done.1
  59.3 0.8 constant_dynamic-update-slice_fusion.3
  60.2 0.9 constant_dynamic-update-slice_fusion.2
  61.0 1.9 %constant_dynamic-update-slice_fusion.1 = bf16[1024,2048]{1,0:T(8,128)(2,1)} fusion(bf16[1024,2048]{1,0:T(8,128)(2,1)} %constant_dynamic-update-slice_fusion.2, bf16[128,2048]{1,0:T(8,128)(2,1)} %collective-permute-done.1), kind=kLoop, calls=%fused_computation.8 | loop fusion | bytes 1048576
  62.9 1.9 %constant_dynamic-update-slice_fusion = bf16[1024,2048]{1,0:T(8,128)(2,1)} fusion(bf16[1024,2048]{1,0:T(8,128)(2,1)} %constant_dynamic-update-slice_fusion.1, bf16[128,2048]{1,0:T(8,128)(2,1)} %collective-permute-done.2), kind=kLoop, calls=%fused_computation.7 | loop fusion | bytes 1048576 | tf_op jit(solution)/shard_map/jit(_roll_dynamic)/concatenate | solution.py:18
  64.8 3.2 %constant_dynamic-slice_fusion = bf16[512,2048]{1,0:T(8,128)(2,1)} fusion(bf16[1024,2048]{1,0:T(8,128)(2,1)} %constant_dynamic-update-slice_fusion, s32[]{:T(128)S(6)} %select_n.19), kind=kLoop, calls=%fused_computation.20 | loop fusion | bytes 4194308 | tf_op jit(solution)/shard_map/jit(_roll_dynamic)/dynamic_slice | solution.py:18
  68.0 3.6 %gather_fusion = bf16[4,128,2048]{2,1,0:T(8,128)(2,1)} fusion(bf16[4,128,2048]{2,1,0:T(8,128)(2,1)} %bitcast.26, s32[1024]{0:T(1024)S(1)} %pad_clamp_fusion), kind=kCustom, calls=%fused_computation | custom fusion | bytes 4194320 | tf_op jit(solution)/shard_map/gather | solution.py:37
  71.6 0.1 broadcast_in_dim.16
  71.7 0.0 copy-done
  71.7 3.9 %fusion.5 = f32[512,512]{1,0:T(8,128)} fusion(f32[512,512]{1,0:T(8,128)S(1)} %bitcast.29, bf16[512,2048]{1,0:T(8,128)(2,1)} %bitcast.27, bf16[1,512,2048]{2,1,0:T(8,128)(2,1)S(1)} %copy-done, f32[512]{0:T(512)S(1)} %bitcast_convert_fusion), kind=kOutput, calls=%fused_computation.6 | convolution fusion | flops 1074266112 | bytes 6293504 | tf_op jit(solution)/shard_map/dot_general | solution.py:41
  75.6 0.0 reduce-scatter.2.cloned.1.call-update
  75.6 20.3 %reduce-scatter.2.cloned.1.call-done = f32[256,512]{1,0:T(8,128)} async-done(((f32[512,512]{1,0:T(8,128)}), f32[256,512]{1,0:T(8,128)}) %reduce-scatter.2.cloned.1.call-update) | async-done | bytes 524304 | tf_op jit(solution)/shard_map/reduce_scatter | solution.py:45
  95.9 2.0 %copy.8 = f32[512,256]{1,0:T(8,128)} copy(f32[512,256]{0,1:T(8,128)} %bitcast.31) | data formatting | bytes 1048576 | tf_op jit(solution)/shard_map/transpose | solution.py:48
  (6 shorter events, 0.0 us)
Async XLA Ops:
  6.5 65.2 %copy-start = (bf16[1,512,2048]{2,1,0:T(8,128)(2,1)S(1)}, bf16[1,512,2048]{2,1,0:T(8,128)(2,1)}, u32[]{:S(2)}) copy-start(bf16[1,512,2048]{2,1,0:T(8,128)(2,1)} %param.5) | copy-start | bytes 6291460
  6.5 52.8 %copy-start.1 = (bf16[1,128,2048]{2,1,0:T(8,128)(2,1)S(1)}, bf16[1,128,2048]{2,1,0:T(8,128)(2,1)}, u32[]{:S(2)}) copy-start(bf16[1,128,2048]{2,1,0:T(8,128)(2,1)} %param.6) | copy-start | bytes 1572868
  6.5 89.3 %reduce-scatter.2.cloned.1.call-start = ((), (), s32[]{:S(2)}) async-start(), calls=%async_computation.1 | async-start | bytes 1572864 | tf_op jit(solution)/shard_map/reduce_scatter | solution.py:45
  6.5 16.6 %collective-permute-start = (bf16[128,2048]{1,0:T(8,128)(2,1)}, bf16[128,2048]{1,0:T(8,128)(2,1)S(1)}, u32[]{:S(2)}, u32[]{:S(2)}) collective-permute-start(bf16[128,2048]{1,0:T(8,128)(2,1)} %bitcast.28), channel_id=1, source_target_pairs={{0,12},{4,0},{8,4},{12,8},{1,13},{5,1},{9,5},{13,9},{2,14},{6,2},{... | collective-permute-start | bytes 1572872 | tf_op jit(solution)/shard_map/ppermute | solution.py:15
  23.1 22.9 %collective-permute-start.1 = (bf16[128,2048]{1,0:T(8,128)(2,1)S(1)}, bf16[128,2048]{1,0:T(8,128)(2,1)}, u32[]{:S(2)}, u32[]{:S(2)}) collective-permute-start(bf16[128,2048]{1,0:T(8,128)(2,1)S(1)} %collective-permute-done), channel_id=1, source_target_pairs={{0,12},{4,0},{8,4},{12,8},{1,13},{5,1},{9,5},{13,9},{2,14},{6,2},{... | collective-permute-start | bytes 1572872 | tf_op jit(solution)/shard_map/ppermute | solution.py:15
  46.0 11.4 %collective-permute-start.2 = (bf16[128,2048]{1,0:T(8,128)(2,1)}, bf16[128,2048]{1,0:T(8,128)(2,1)}, u32[]{:S(2)}, u32[]{:S(2)}) collective-permute-start(bf16[128,2048]{1,0:T(8,128)(2,1)} %collective-permute-done.1), channel_id=1, source_target_pairs={{0,12},{4,0},{8,4},{12,8},{1,13},{5,1},{9,5},{13,9},{2,14},{6,2},{... | collective-permute-start | bytes 1572872 | tf_op jit(solution)/shard_map/ppermute | solution.py:15
Sparse Core Ops, SparseCore 0:
  75.7 20.0 reduce-scatter.1
